TPU v7x, 256 devices: a whole 4x4x8 slice. The times are simulated.
256 devices in a mesh: row: 16 (over z, core), col: 16 (over y, x).
Axes of the slice: x: 4, y: 4, z: 8, core: 2. Of those that a mesh axis runs over, the one named last changes fastest.
Arguments:
- start_block: float32 [4096, 64, 128], P(('row', 'col')), may hold values from -2700 to 2700
- tile_values: bfloat16 [65536, 128, 128], P(('row', 'col')), may hold values from -3.535534 to 3.535534
- tile_rows: int32 [65536], P(('row', 'col')), may hold values from 0 to 15
- tile_cols: int32 [65536], P(('row', 'col')), may hold values from 0 to 79
- tile_count: int32 [256], P(('row', 'col')), may hold values from 32 to 256, as said below
- send_rows: int32 [256, 256, 32], P(('row', 'col')), may hold values from 0 to 2047
- send_count: int32 [256, 256], P(('row', 'col')), may hold values from 16 to 32, as said below
- rotation: float32 [192, 64], replicated, may hold values from -0.4375 to 0.4375
Outputs:
- embedding: float32 [4096, 64, 128], P(('row', 'col'))
Inputs may be any that keep to these rules, and one draw needn't show every extreme that they name: `tile_cols`: source tiles below 16 are the partition's own row tiles, the others its halo tiles. `tile_count`: slots at or past the count are ignored; some partition fills all 256 slots. `send_count`: slots at or past the count carry zeros; every partition fills all 32 slots for some peer, and some partition receives 32 rows from every partition.
All inputs are finite; a program needn't handle non-finite values.
Results may differ from a plain program's by a relative error of at most 0.0029.
Values may be sent and summed in bfloat16 or wider, within the bound.
A program may use at most 64 MiB of HBM per device.

v0:
```python
import jax
import jax.numpy as jnp
from jax import lax
from jax.sharding import PartitionSpec as P

HIGHEST_PRECISION = lax.Precision.HIGHEST


def local_inner(left_block, right_block):
    return jnp.einsum("tai,tbi->ab", left_block, right_block, precision=HIGHEST_PRECISION)


def unit_columns(product_block, gram_matrix):
    factor = jnp.linalg.cholesky(gram_matrix)
    inverse = lax.linalg.triangular_solve(
        factor, jnp.eye(factor.shape[0], dtype=jnp.float32), left_side=True, lower=True
    )
    return jnp.einsum("ab,tbi->tai", inverse, product_block, precision=HIGHEST_PRECISION)


def apply_graph(current, tile_values, tile_rows, tile_cols, tile_count, send_rows, send_count):
    row_tiles, block_width, tile_size = current.shape
    rounded = current.astype(jnp.bfloat16)
    node_rows = rounded.transpose(0, 2, 1).reshape(row_tiles * tile_size, block_width)
    targets = send_rows[0]
    partitions, capacity = targets.shape
    chosen = node_rows[targets.reshape(-1)].reshape(partitions, capacity, block_width)
    kept_slots = jnp.arange(capacity, dtype=jnp.int32)[None, :] < send_count[0][:, None]
    chosen = jnp.where(kept_slots[:, :, None], chosen, jnp.zeros_like(chosen))
    outgoing = chosen.reshape(lax.axis_size("row"), lax.axis_size("col"), capacity * block_width)
    incoming = lax.all_to_all(
        lax.all_to_all(outgoing, "row", split_axis=0, concat_axis=0, tiled=True),
        "col",
        split_axis=1,
        concat_axis=1,
        tiled=True,
    )
    halo_count = partitions * capacity // tile_size
    halo_block = incoming.reshape(halo_count, tile_size, block_width).transpose(0, 2, 1)
    source = jnp.concatenate([rounded, halo_block], 0)
    picked = source[tile_cols]
    products = jnp.einsum("kbj,kij->kbi", picked, tile_values, preferred_element_type=jnp.float32)
    slot_total = tile_cols.shape[0]
    live_slots = jnp.arange(slot_total, dtype=jnp.int32) < tile_count[0]
    owner_table = (
        tile_rows[None, :] == jnp.arange(row_tiles, dtype=jnp.int32)[:, None]
    ) & live_slots[None, :]
    return jnp.einsum(
        "rk,kbi->rbi", owner_table.astype(jnp.float32), products, precision=HIGHEST_PRECISION
    )


def body(
    start_block, tile_values, tile_rows, tile_cols, tile_count, send_rows, send_count, rotation
):
    node_total = (
        start_block.shape[0] * start_block.shape[2] * lax.axis_size("row") * lax.axis_size("col")
    )
    start_sum = lax.psum(local_inner(start_block, start_block), ("row", "col"))
    vectors = [unit_columns(start_block, start_sum / node_total)]
    for krylov_step in range(2):
        product_block = apply_graph(
            vectors[-1], tile_values, tile_rows, tile_cols, tile_count, send_rows, send_count
        )
        stacked = jnp.concatenate(vectors, 1)
        coefficients = lax.psum(local_inner(stacked, product_block), ("row", "col")) / node_total
        residual_block = product_block - jnp.einsum(
            "ab,tai->tbi", coefficients, stacked, precision=HIGHEST_PRECISION
        )
        gram_matrix = (
            lax.psum(local_inner(residual_block, residual_block), ("row", "col")) / node_total
        )
        vectors.append(unit_columns(residual_block, gram_matrix))
    all_vectors = jnp.concatenate(vectors, 1)
    return jnp.einsum("jb,tji->tbi", rotation, all_vectors, precision=HIGHEST_PRECISION)


def solution(mesh):
    return jax.shard_map(
        body,
        mesh=mesh,
        in_specs=(
            P(("row", "col"), None, None),
            P(("row", "col"), None, None),
            P(("row", "col")),
            P(("row", "col")),
            P(("row", "col")),
            P(("row", "col"), None, None),
            P(("row", "col"), None),
            P(),
        ),
        out_specs=P(("row", "col"), None, None),
        check_vma=False,
    )
```

profile of v0, /device:TPU:1, one launch (start us, length us, event | category | flops | bytes accessed | tf_op | source)
XLA Modules:
  0.0 668.5 jit_solution(7324829424072807957)
XLA Ops:
  1.6 81.5 %psum.35 = f32[64,64]{0,1:T(8,128)S(1)} all-reduce(f32[64,64]{0,1:T(8,128)S(1)} %convolution_bitcast_fusion.8), channel_id=1, replica_groups=mesh['row'=16,'col'=16] {'row','col'}, use_global_device_ids=true, to_apply=%region_0.0 | all-reduce | flops 4096 | bytes 32768 | tf_op jit(solution)/shard_map/psum | solution.py:59
  83.2 5.8 cholesky.59
  90.4 4.9 custom-call.7
  96.8 24.0 %gather_fusion = bf16[8192,64]{1,0:T(8,128)(2,1)S(1)} fusion(bf16[2048,64]{1,0:T(8,128)(2,1)S(1)} %bitcast.92, s32[8192]{0:T(1024)S(1)} %broadcast_clamp_fusion), kind=kCustom, calls=%fused_computation | custom fusion | bytes 2129920 | tf_op jit(solution)/shard_map/gather | solution.py:27
  120.9 2.4 reshape.93
  123.4 2.1 broadcast_in_dim.16
  128.8 33.5 %all_to_all.20 = bf16[16,16,2048]{2,1,0:T(8,128)(2,1)S(1)} all-to-all(bf16[16,16,2048]{2,1,0:T(8,128)(2,1)S(1)} %broadcast_select_fusion.1), channel_id=1, replica_groups=mesh['row'=16,'col'=16] {'row'}, dimensions={0} | all-to-all | bytes 2097152 | tf_op jit(solution)/shard_map/all_to_all | solution.py:32
  163.9 3.9 all-to-all-start.1
  168.7 16.5 %all-to-all-done.1 = bf16[16,16,2048]{2,0,1:T(8,128)(2,1)S(1)} async-done(((bf16[16,16,2048]{2,0,1:T(8,128)(2,1)}), bf16[16,16,2048]{2,0,1:T(8,128)(2,1)S(1)}, u32[]{:S(2)}, u32[]{:S(2)}) %all-to-all-start.1) | async-done | bytes 1048608 | tf_op jit(solution)/shard_map/all_to_all | solution.py:31
  186.8 3.3 reshape.94
  190.2 2.1 pad_maximum_fusion
  192.2 10.4 %gather_fusion.1 = bf16[256,64,128]{1,2,0:T(8,128)(2,1)} fusion(bf16[80,64,128]{1,2,0:T(8,128)(2,1)} %pad_maximum_fusion, s32[1024]{0:T(1024)S(1)} %pad_clamp_fusion), kind=kCustom, calls=%fused_computation.1 | custom fusion | bytes 8389632 | tf_op jit(solution)/shard_map/gather | solution.py:41
  202.6 9.7 %fusion.57 = f32[256,64,128]{2,1,0:T(8,128)S(1)} fusion(bf16[256,64,128]{1,2,0:T(8,128)(2,1)} %gather_fusion.1, bf16[256,128,128]{2,1,0:T(8,128)(2,1)} %param.12), kind=kOutput, calls=%fused_computation.100 | convolution fusion | flops 536870912 | bytes 20971520 | tf_op jit(solution)/shard_map/kbj,kij->kbi/dot_general | solution.py:42
  212.3 7.5 %fusion.2 = f32[16,64,128]{2,0,1:T(8,128)S(1)} fusion(f32[256,64,128]{2,1,0:T(8,128)S(1)} %fusion.57, s32[256]{0:T(256)S(1)} %copy-done.6, pred[256]{0:T(512)(128)(4,1)S(1)} %iota_compare_fusion.7), kind=kOutput, calls=%fused_computation.6 | convolution fusion | flops 402661376 | bytes 8914176 | tf_op jit(solution)/shard_map/rk,kbi->rbi/dot_general | solution.py:48
  220.5 72.7 %psum.36 = f32[64,64]{0,1:T(8,128)S(1)} all-reduce(f32[64,64]{0,1:T(8,128)S(1)} %convolution_bitcast_fusion.6), channel_id=1, replica_groups=mesh['row'=16,'col'=16] {'row','col'}, use_global_device_ids=true, to_apply=%region_3.0 | all-reduce | flops 4096 | bytes 32768 | tf_op jit(solution)/shard_map/psum | solution.py:66
  295.0 73.9 %psum.37 = f32[64,64]{0,1:T(8,128)S(1)} all-reduce(f32[64,64]{0,1:T(8,128)S(1)} %convolution_bitcast_fusion.5), channel_id=1, replica_groups=mesh['row'=16,'col'=16] {'row','col'}, use_global_device_ids=true, to_apply=%region_4.0 | all-reduce | flops 4096 | bytes 32768 | tf_op jit(solution)/shard_map/psum | solution.py:71
  369.0 5.8 cholesky.70
  376.3 4.9 custom-call.8
  383.3 24.0 %gather_fusion.2 = bf16[8192,64]{1,0:T(8,128)(2,1)S(1)} fusion(bf16[2048,64]{1,0:T(8,128)(2,1)S(1)} %bitcast.93, s32[8192]{0:T(1024)S(1)} %broadcast_clamp_fusion), kind=kCustom, calls=%fused_computation.2 | custom fusion | bytes 2129920 | tf_op jit(solution)/shard_map/gather | solution.py:27
  407.4 2.4 reshape.96
  411.3 32.6 %all_to_all.21 = bf16[16,16,2048]{2,1,0:T(8,128)(2,1)S(1)} all-to-all(bf16[16,16,2048]{2,1,0:T(8,128)(2,1)S(1)} %broadcast_select_fusion), channel_id=1, replica_groups=mesh['row'=16,'col'=16] {'row'}, dimensions={0} | all-to-all | bytes 2097152 | tf_op jit(solution)/shard_map/all_to_all | solution.py:32
  445.5 3.9 all-to-all-start.3
  449.7 18.4 %all-to-all-done.3 = bf16[16,16,2048]{2,0,1:T(8,128)(2,1)S(1)} async-done(((bf16[16,16,2048]{2,0,1:T(8,128)(2,1)}), bf16[16,16,2048]{2,0,1:T(8,128)(2,1)S(1)}, u32[]{:S(2)}, u32[]{:S(2)}) %all-to-all-start.3) | async-done | bytes 1048608 | tf_op jit(solution)/shard_map/all_to_all | solution.py:31
  469.7 3.3 reshape.97
  473.0 2.1 pad_maximum_fusion.1
  475.1 10.4 %gather_fusion.3 = bf16[256,64,128]{1,2,0:T(8,128)(2,1)} fusion(bf16[80,64,128]{1,2,0:T(8,128)(2,1)} %pad_maximum_fusion.1, s32[1024]{0:T(1024)S(1)} %pad_clamp_fusion), kind=kCustom, calls=%fused_computation.3 | custom fusion | bytes 8389632 | tf_op jit(solution)/shard_map/gather | solution.py:41
  485.5 9.5 %fusion.58 = f32[256,64,128]{2,1,0:T(8,128)S(1)} fusion(bf16[256,64,128]{1,2,0:T(8,128)(2,1)} %gather_fusion.3, bf16[256,128,128]{2,1,0:T(8,128)(2,1)} %param.12), kind=kOutput, calls=%fused_computation.101 | convolution fusion | flops 536870912 | bytes 20971520 | tf_op jit(solution)/shard_map/kbj,kij->kbi/dot_general | solution.py:42
  495.0 7.5 %fusion = f32[16,64,128]{2,0,1:T(8,128)S(1)} fusion(f32[256,64,128]{2,1,0:T(8,128)S(1)} %fusion.58, s32[256]{0:T(256)S(1)} %copy-done.6, pred[256]{0:T(512)(128)(4,1)S(1)} %iota_compare_fusion.7), kind=kOutput, calls=%fused_computation.4 | convolution fusion | flops 402661376 | bytes 8914176 | tf_op jit(solution)/shard_map/rk,kbi->rbi/dot_general | solution.py:48
  503.7 72.8 %psum.38 = f32[128,64]{0,1:T(8,128)S(1)} all-reduce(f32[128,64]{0,1:T(8,128)S(1)} %convolution_bitcast_fusion.1), channel_id=1, replica_groups=mesh['row'=16,'col'=16] {'row','col'}, use_global_device_ids=true, to_apply=%region_5.8 | all-reduce | flops 8192 | bytes 65536 | tf_op jit(solution)/shard_map/psum | solution.py:66
  578.3 74.5 %psum.39 = f32[64,64]{0,1:T(8,128)S(1)} all-reduce(f32[64,64]{0,1:T(8,128)S(1)} %convolution_bitcast_fusion.3), channel_id=1, replica_groups=mesh['row'=16,'col'=16] {'row','col'}, use_global_device_ids=true, to_apply=%region_6.9 | all-reduce | flops 4096 | bytes 32768 | tf_op jit(solution)/shard_map/psum | solution.py:71
  652.9 5.8 cholesky.81
  660.1 4.9 custom-call.9
  (72 shorter events, 29.6 us)
Async XLA Ops:
  0.0 1.0 copy-start
  0.0 96.5 %copy-start.5 = (s32[1,256,32]{1,2,0:T(8,128)S(1)}, s32[1,256,32]{1,2,0:T(8,128)}, u32[]{:S(2)}) copy-start(s32[1,256,32]{1,2,0:T(8,128)} %param.16) | copy-start | bytes 98308
  96.8 26.5 %copy-start.7 = (s32[1,256]{1,0:T(1,128)S(1)}, s32[1,256]{1,0:T(1,128)}, u32[]{:S(2)}) copy-start(s32[1,256]{1,0:T(1,128)} %param.17) | copy-start | bytes 3076
  127.3 36.6 %copy-start.3 = (pred[16,16,2048]{2,1,0:T(8,128)(4,1)}, pred[16,16,2048]{2,1,0:T(8,128)(4,1)S(1)}, u32[]{:S(2)}) copy-start(pred[16,16,2048]{2,1,0:T(8,128)(4,1)S(1)} %broadcast_in_dim.17) | copy-start | bytes 1572868
  128.8 39.9 %copy-start.8 = (s32[256]{0:T(256)S(1)}, s32[256]{0:T(256)}, u32[]{:S(2)}) copy-start(s32[256]{0:T(256)} %param.14) | copy-start | bytes 3076
  163.9 21.4 %all-to-all-start.1 = ((bf16[16,16,2048]{2,0,1:T(8,128)(2,1)}), bf16[16,16,2048]{2,0,1:T(8,128)(2,1)S(1)}, u32[]{:S(2)}, u32[]{:S(2)}) async-start(bf16[16,16,2048]{2,0,1:T(8,128)(2,1)} %copy.49), calls=%async_computation.1 | async-start | bytes 2097152 | tf_op jit(solution)/shard_map/all_to_all | solution.py:31
  202.6 9.7 %copy-start.6 = (s32[256]{0:T(256)S(1)}, s32[256]{0:T(256)}, u32[]{:S(2)}) copy-start(s32[256]{0:T(256)} %param.13) | copy-start | bytes 3076
  445.5 22.6 %all-to-all-start.3 = ((bf16[16,16,2048]{2,0,1:T(8,128)(2,1)}), bf16[16,16,2048]{2,0,1:T(8,128)(2,1)S(1)}, u32[]{:S(2)}, u32[]{:S(2)}) async-start(bf16[16,16,2048]{2,0,1:T(8,128)(2,1)} %copy.64), calls=%async_computation.3 | async-start | bytes 2097152 | tf_op jit(solution)/shard_map/all_to_all | solution.py:31
  495.0 7.5 %copy-start.2 = (f32[16,128,64]{1,2,0:T(8,128)S(1)}, f32[16,128,64]{1,2,0:T(8,128)}, u32[]{:S(2)}) copy-start(f32[16,128,64]{1,2,0:T(8,128)} %get-tuple-element.11) | copy-start | bytes 1572868
  502.5 163.6 %copy-start.4 = (f32[192,64]{0,1:T(8,128)S(1)}, f32[192,64]{0,1:T(8,128)}, u32[]{:S(2)}) copy-start(f32[192,64]{0,1:T(8,128)} %param.18) | copy-start | bytes 147460
  502.5 165.5 %copy-start.1 = (f32[16,64,128]{2,1,0:T(8,128)S(1)}, f32[16,64,128]{2,1,0:T(8,128)}, u32[]{:S(2)}) copy-start(f32[16,64,128]{2,1,0:T(8,128)} %param.11) | copy-start | bytes 1572868
where the time goes:
time: 675 us; the launch traced here: 668 us
  blocking collectives  442 us (65%)
  local copies, waits for them, and re-layouts  93.1 us (14%)
  matrix products  45.1 us (7%)
  other arithmetic  44.5 us (7%)
  waiting for transfers between devices  35 us (5%)
  starting transfers between devices  7.75 us (1%)
    psum x2, blocking collectives, body(): lax.psum(local_inner(residual_block, residual_block), ('row', 'col'))  148 us
    psum x2, blocking collectives, body(): lax.psum(local_inner(stacked, product_block), ('row', 'col')) / node_total  146 us
    psum x1, blocking collectives, body(): start_sum = lax.psum(local_inner(start_block, start_block), ('row', 'col'))  81.5 us
    all_to_all x2, blocking collectives, apply_graph(): lax.all_to_all(outgoing, 'row', split_axis=0, concat_axis=0, tiled=True)  66.1 us
    gather x2, local copies, waits for them, and re-layouts, apply_graph(): node_rows[targets.reshape(-1)].reshape(partitions, capacity, block_width)  48.1 us
    all_to_all x2, waiting for transfers between devices, apply_graph(): lax.all_to_all(lax.all_to_all(outgoing, 'row', split_axis=0, concat_axis=...  35 us
    gather x2, local copies, waits for them, and re-layouts, apply_graph(): picked = source[tile_cols]  20.7 us
    another operation x9, other arithmetic, unit_columns(): factor = jnp.linalg.cholesky(gram_matrix)  19.6 us
  transfers between devices with their start and end apart: 2, of which 2 were waited for; matrix products, arithmetic and copies ran while one was open for 0% of the time, Pallas kernels for 0%

commit v1 on v0

--- a/solution.py
+++ b/solution.py
@@ -63,7 +63,9 @@
             vectors[-1], tile_values, tile_rows, tile_cols, tile_count, send_rows, send_count
         )
         stacked = jnp.concatenate(vectors, 1)
-        coefficients = lax.psum(local_inner(stacked, product_block), ("row", "col")) / node_total
+        coefficients = (
+            lax.psum(lax.psum(local_inner(stacked, product_block), "col"), "row") / node_total
+        )
         residual_block = product_block - jnp.einsum(
             "ab,tai->tbi", coefficients, stacked, precision=HIGHEST_PRECISION
         )

time: 675 us -> 756 us (1.12)
  blocking collectives: 442 us -> 522 us
    psum x2 -> x4, blocking collectives: 146 us -> 224 us  [the longest x2 112 us: body(): lax.psum(local_inner(stacked, product_block), 'col')]
where the time goes in v1:
time: 756 us; the launch traced here: 749 us
  blocking collectives  522 us (69%)
  local copies, waits for them, and re-layouts  93.1 us (12%)
  matrix products  45.1 us (6%)
  other arithmetic  44.5 us (6%)
  waiting for transfers between devices  35 us (5%)
  starting transfers between devices  8.1 us (1%)
    psum x2, blocking collectives, body(): lax.psum(local_inner(residual_block, residual_block), ('row', 'col'))  149 us
    psum x2, blocking collectives, body(): lax.psum(local_inner(stacked, product_block), 'col')  112 us
    psum x2, blocking collectives, body(): lax.psum(lax.psum(local_inner(stacked, product_block), 'col'), 'row')  112 us
    psum x1, blocking collectives, body(): start_sum = lax.psum(local_inner(start_block, start_block), ('row', 'col'))  81.5 us
    all_to_all x2, blocking collectives, apply_graph(): lax.all_to_all(outgoing, 'row', split_axis=0, concat_axis=0, tiled=True)  67.3 us
    gather x2, local copies, waits for them, and re-layouts, apply_graph(): node_rows[targets.reshape(-1)].reshape(partitions, capacity, block_width)  48.1 us
    all_to_all x2, waiting for transfers between devices, apply_graph(): lax.all_to_all(lax.all_to_all(outgoing, 'row', split_axis=0, concat_axis=...  35 us
    gather x2, local copies, waits for them, and re-layouts, apply_graph(): picked = source[tile_cols]  20.7 us
  transfers between devices with their start and end apart: 2, of which 2 were waited for; matrix products, arithmetic and copies ran while one was open for 0% of the time, Pallas kernels for 0%

profile of v1, /device:TPU:1, one launch (start us, length us, event | category | flops | bytes accessed | tf_op | source)
XLA Modules:
  0.0 749.2 jit_solution(14155034040641540181)
XLA Ops:
  1.6 81.5 %psum.49 = f32[64,64]{0,1:T(8,128)S(1)} all-reduce(f32[64,64]{0,1:T(8,128)S(1)} %convolution_bitcast_fusion.8), channel_id=1, replica_groups=mesh['row'=16,'col'=16] {'row','col'}, use_global_device_ids=true, to_apply=%region_0.0 | all-reduce | flops 4096 | bytes 32768 | tf_op jit(solution)/shard_map/psum | solution.py:59
  83.2 5.8 cholesky.59
  90.4 4.9 custom-call.7
  96.8 24.0 %gather_fusion = bf16[8192,64]{1,0:T(8,128)(2,1)S(1)} fusion(bf16[2048,64]{1,0:T(8,128)(2,1)S(1)} %bitcast.92, s32[8192]{0:T(1024)S(1)} %broadcast_clamp_fusion), kind=kCustom, calls=%fused_computation | custom fusion | bytes 2129920 | tf_op jit(solution)/shard_map/gather | solution.py:27
  120.9 2.4 reshape.93
  128.8 33.5 %all_to_all.20 = bf16[16,16,2048]{2,1,0:T(8,128)(2,1)S(1)} all-to-all(bf16[16,16,2048]{2,1,0:T(8,128)(2,1)S(1)} %broadcast_select_fusion.1), channel_id=1, replica_groups=mesh['row'=16,'col'=16] {'row'}, dimensions={0} | all-to-all | bytes 2097152 | tf_op jit(solution)/shard_map/all_to_all | solution.py:32
  163.9 3.9 all-to-all-start.1
  168.7 16.5 %all-to-all-done.1 = bf16[16,16,2048]{2,0,1:T(8,128)(2,1)S(1)} async-done(((bf16[16,16,2048]{2,0,1:T(8,128)(2,1)}), bf16[16,16,2048]{2,0,1:T(8,128)(2,1)S(1)}, u32[]{:S(2)}, u32[]{:S(2)}) %all-to-all-start.1) | async-done | bytes 1048608 | tf_op jit(solution)/shard_map/all_to_all | solution.py:31
  186.8 3.3 reshape.94
  190.2 2.1 pad_maximum_fusion
  192.2 10.4 %gather_fusion.1 = bf16[256,64,128]{1,2,0:T(8,128)(2,1)} fusion(bf16[80,64,128]{1,2,0:T(8,128)(2,1)} %pad_maximum_fusion, s32[1024]{0:T(1024)S(1)} %pad_clamp_fusion), kind=kCustom, calls=%fused_computation.1 | custom fusion | bytes 8389632 | tf_op jit(solution)/shard_map/gather | solution.py:41
  202.6 9.7 %fusion.57 = f32[256,64,128]{2,1,0:T(8,128)S(1)} fusion(bf16[256,64,128]{1,2,0:T(8,128)(2,1)} %gather_fusion.1, bf16[256,128,128]{2,1,0:T(8,128)(2,1)} %param.12), kind=kOutput, calls=%fused_computation.100 | convolution fusion | flops 536870912 | bytes 20971520 | tf_op jit(solution)/shard_map/kbj,kij->kbi/dot_general | solution.py:42
  212.3 7.5 %fusion.2 = f32[16,64,128]{2,0,1:T(8,128)S(1)} fusion(f32[256,64,128]{2,1,0:T(8,128)S(1)} %fusion.57, s32[256]{0:T(256)S(1)} %copy-done.6, pred[256]{0:T(512)(128)(4,1)S(1)} %iota_compare_fusion.7), kind=kOutput, calls=%fused_computation.6 | convolution fusion | flops 402661376 | bytes 8914176 | tf_op jit(solution)/shard_map/rk,kbi->rbi/dot_general | solution.py:48
  220.5 56.5 %psum.50 = f32[64,64]{0,1:T(8,128)S(1)} all-reduce(f32[64,64]{0,1:T(8,128)S(1)} %convolution_bitcast_fusion.6), channel_id=1, replica_groups=mesh['row'=16,'col'=16] {'col'}, use_global_device_ids=true, to_apply=%region_3.0 | all-reduce | flops 4096 | bytes 32768 | tf_op jit(solution)/shard_map/psum | solution.py:67
  277.1 55.4 %psum.51 = f32[64,64]{0,1:T(8,128)S(1)} all-reduce(f32[64,64]{0,1:T(8,128)S(1)} %psum.50), channel_id=1, replica_groups=mesh['row'=16,'col'=16] {'row'}, use_global_device_ids=true, to_apply=%region_4.0 | all-reduce | flops 4096 | bytes 32768 | tf_op jit(solution)/shard_map/psum | solution.py:67
  334.2 74.6 %psum.52 = f32[64,64]{0,1:T(8,128)S(1)} all-reduce(f32[64,64]{0,1:T(8,128)S(1)} %convolution_bitcast_fusion.5), channel_id=1, replica_groups=mesh['row'=16,'col'=16] {'row','col'}, use_global_device_ids=true, to_apply=%region_5.0 | all-reduce | flops 4096 | bytes 32768 | tf_op jit(solution)/shard_map/psum | solution.py:73
  408.9 5.8 cholesky.70
  416.2 4.9 custom-call.8
  423.2 24.0 %gather_fusion.2 = bf16[8192,64]{1,0:T(8,128)(2,1)S(1)} fusion(bf16[2048,64]{1,0:T(8,128)(2,1)S(1)} %bitcast.93, s32[8192]{0:T(1024)S(1)} %broadcast_clamp_fusion), kind=kCustom, calls=%fused_computation.2 | custom fusion | bytes 2129920 | tf_op jit(solution)/shard_map/gather | solution.py:27
  447.3 2.4 reshape.96
  451.2 33.8 %all_to_all.21 = bf16[16,16,2048]{2,1,0:T(8,128)(2,1)S(1)} all-to-all(bf16[16,16,2048]{2,1,0:T(8,128)(2,1)S(1)} %broadcast_select_fusion), channel_id=1, replica_groups=mesh['row'=16,'col'=16] {'row'}, dimensions={0} | all-to-all | bytes 2097152 | tf_op jit(solution)/shard_map/all_to_all | solution.py:32
  486.6 4.2 all-to-all-start.3
  491.1 18.4 %all-to-all-done.3 = bf16[16,16,2048]{2,0,1:T(8,128)(2,1)S(1)} async-done(((bf16[16,16,2048]{2,0,1:T(8,128)(2,1)}), bf16[16,16,2048]{2,0,1:T(8,128)(2,1)S(1)}, u32[]{:S(2)}, u32[]{:S(2)}) %all-to-all-start.3) | async-done | bytes 1048608 | tf_op jit(solution)/shard_map/all_to_all | solution.py:31
  511.1 3.3 reshape.97
  516.6 10.4 %gather_fusion.3 = bf16[256,64,128]{1,2,0:T(8,128)(2,1)} fusion(bf16[80,64,128]{1,2,0:T(8,128)(2,1)} %pad_maximum_fusion.1, s32[1024]{0:T(1024)S(1)} %pad_clamp_fusion), kind=kCustom, calls=%fused_computation.3 | custom fusion | bytes 8389632 | tf_op jit(solution)/shard_map/gather | solution.py:41
  526.9 9.5 %fusion.58 = f32[256,64,128]{2,1,0:T(8,128)S(1)} fusion(bf16[256,64,128]{1,2,0:T(8,128)(2,1)} %gather_fusion.3, bf16[256,128,128]{2,1,0:T(8,128)(2,1)} %param.12), kind=kOutput, calls=%fused_computation.101 | convolution fusion | flops 536870912 | bytes 20971520 | tf_op jit(solution)/shard_map/kbj,kij->kbi/dot_general | solution.py:42
  536.4 7.5 %fusion = f32[16,64,128]{2,0,1:T(8,128)S(1)} fusion(f32[256,64,128]{2,1,0:T(8,128)S(1)} %fusion.58, s32[256]{0:T(256)S(1)} %copy-done.6, pred[256]{0:T(512)(128)(4,1)S(1)} %iota_compare_fusion.7), kind=kOutput, calls=%fused_computation.4 | convolution fusion | flops 402661376 | bytes 8914176 | tf_op jit(solution)/shard_map/rk,kbi->rbi/dot_general | solution.py:48
  545.1 55.9 %psum.53 = f32[128,64]{0,1:T(8,128)S(1)} all-reduce(f32[128,64]{0,1:T(8,128)S(1)} %convolution_bitcast_fusion.1), channel_id=1, replica_groups=mesh['row'=16,'col'=16] {'col'}, use_global_device_ids=true, to_apply=%region_6.0 | all-reduce | flops 8192 | bytes 65536 | tf_op jit(solution)/shard_map/psum | solution.py:67
  601.0 56.1 %psum.54 = f32[128,64]{0,1:T(8,128)S(1)} all-reduce(f32[128,64]{0,1:T(8,128)S(1)} %psum.53), channel_id=1, replica_groups=mesh['row'=16,'col'=16] {'row'}, use_global_device_ids=true, to_apply=%region_7.10 | all-reduce | flops 8192 | bytes 65536 | tf_op jit(solution)/shard_map/psum | solution.py:67
  658.9 74.7 %psum.55 = f32[64,64]{0,1:T(8,128)S(1)} all-reduce(f32[64,64]{0,1:T(8,128)S(1)} %convolution_bitcast_fusion.3), channel_id=1, replica_groups=mesh['row'=16,'col'=16] {'row','col'}, use_global_device_ids=true, to_apply=%region_8.11 | all-reduce | flops 4096 | bytes 32768 | tf_op jit(solution)/shard_map/psum | solution.py:73
  733.7 5.8 cholesky.81
  740.9 4.9 custom-call.9
  (74 shorter events, 33.8 us)
Async XLA Ops:
  0.0 1.0 copy-start
  0.0 96.5 %copy-start.5 = (s32[1,256,32]{1,2,0:T(8,128)S(1)}, s32[1,256,32]{1,2,0:T(8,128)}, u32[]{:S(2)}) copy-start(s32[1,256,32]{1,2,0:T(8,128)} %param.16) | copy-start | bytes 98308
  96.8 26.5 %copy-start.7 = (s32[1,256]{1,0:T(1,128)S(1)}, s32[1,256]{1,0:T(1,128)}, u32[]{:S(2)}) copy-start(s32[1,256]{1,0:T(1,128)} %param.17) | copy-start | bytes 3076
  127.3 36.6 %copy-start.3 = (pred[16,16,2048]{2,1,0:T(8,128)(4,1)}, pred[16,16,2048]{2,1,0:T(8,128)(4,1)S(1)}, u32[]{:S(2)}) copy-start(pred[16,16,2048]{2,1,0:T(8,128)(4,1)S(1)} %broadcast_in_dim.17) | copy-start | bytes 1572868
  128.8 39.9 %copy-start.8 = (s32[256]{0:T(256)S(1)}, s32[256]{0:T(256)}, u32[]{:S(2)}) copy-start(s32[256]{0:T(256)} %param.14) | copy-start | bytes 3076
  163.9 21.4 %all-to-all-start.1 = ((bf16[16,16,2048]{2,0,1:T(8,128)(2,1)}), bf16[16,16,2048]{2,0,1:T(8,128)(2,1)S(1)}, u32[]{:S(2)}, u32[]{:S(2)}) async-start(bf16[16,16,2048]{2,0,1:T(8,128)(2,1)} %copy.49), calls=%async_computation.1 | async-start | bytes 2097152 | tf_op jit(solution)/shard_map/all_to_all | solution.py:31
  202.6 9.7 %copy-start.6 = (s32[256]{0:T(256)S(1)}, s32[256]{0:T(256)}, u32[]{:S(2)}) copy-start(s32[256]{0:T(256)} %param.13) | copy-start | bytes 3076
  486.6 23.0 %all-to-all-start.3 = ((bf16[16,16,2048]{2,0,1:T(8,128)(2,1)}), bf16[16,16,2048]{2,0,1:T(8,128)(2,1)S(1)}, u32[]{:S(2)}, u32[]{:S(2)}) async-start(bf16[16,16,2048]{2,0,1:T(8,128)(2,1)} %copy.64), calls=%async_computation.3 | async-start | bytes 2097152 | tf_op jit(solution)/shard_map/all_to_all | solution.py:31
  536.4 7.5 %copy-start.2 = (f32[16,128,64]{1,2,0:T(8,128)S(1)}, f32[16,128,64]{1,2,0:T(8,128)}, u32[]{:S(2)}) copy-start(f32[16,128,64]{1,2,0:T(8,128)} %get-tuple-element.11) | copy-start | bytes 1572868
  543.9 202.9 %copy-start.4 = (f32[192,64]{0,1:T(8,128)S(1)}, f32[192,64]{0,1:T(8,128)}, u32[]{:S(2)}) copy-start(f32[192,64]{0,1:T(8,128)} %param.18) | copy-start | bytes 147460
  544.0 204.8 %copy-start.1 = (f32[16,64,128]{2,1,0:T(8,128)S(1)}, f32[16,64,128]{2,1,0:T(8,128)}, u32[]{:S(2)}) copy-start(f32[16,64,128]{2,1,0:T(8,128)} %param.11) | copy-start | bytes 1572868
